TPU v7x, 256 devices: a whole 4x4x8 slice. The times are simulated.
256 devices in a mesh: lat: 32 (over x_lo, z, core), ch: 8 (over y, x_hi).
Axes of the slice: x: 4 (x_hi: 2, x_lo: 2; x = x_hi * 2 + x_lo), y: 4, z: 8, core: 2. Of those that a mesh axis runs over, the one named last changes fastest.
Arguments:
- spectrum: bfloat16 [512, 64, 2, 2, 256], P('lat', 'ch'), may hold values from -0.01953125 to 0.01953125
- legendre: bfloat16 [640, 256, 512], P('lat'), as said below
- block_slots: int32 [32], replicated, may hold values from 0 to 31, each once
- kernel_values: bfloat16 [3, 640, 6, 9], P(None, 'lat'), may hold values from -2 to 2
- near_rows: int32 [640, 6], P('lat'), may hold values from 0 to 639, as said below
- mix_weights: bfloat16 [3, 64, 64], replicated, may hold values from -0.4375 to 0.4375
Outputs:
- convolved: bfloat16 [64, 640, 1440], P('ch', 'lat')
Inputs may be any that keep to these rules, and one draw needn't show every extreme that they name: legendre[r, k, m] is zero where m + 2 * k + p >= 512, with p = 0 for r < 320 and p = 1 otherwise. near_rows[r, q] lies within 2 rows of r; slot 0 holds max(r - 2, 0) and slot 1 holds min(r + 2, 639). `block_slots`: each order block appears once.
All inputs are finite; a program needn't handle non-finite values.
Results may differ from a plain program's by a relative error of at most 0.005.
Values may be sent and summed in bfloat16 or wider, within the bound.
No kernel may reach another device: no remote copies, remote signals or barrier semaphores. Data moves between devices by JAX's collectives and lax.ppermute only.
A program may use at most 320 MiB of HBM per device.

v0:
```python
import math
import jax
import jax.numpy as jnp
from jax import lax
from jax.sharding import PartitionSpec as P

NLON = 1440
LMAX = 512
ORDER_BLOCK = 16
KER = 3
REACH = 2
LON_REACH = 4
TAPS = 9


def padded_2(shard, sides, width):
    for axis, dim in sides:
        count, length = (lax.axis_size(axis), shard.shape[dim])
        up = [(i, (i + 1) % count) for i in range(count - 1)]
        down = [(j, i) for i, j in up]
        last = lax.slice_in_dim(shard, length - width, length, axis=dim)
        first = lax.slice_in_dim(shard, 0, width, axis=dim)
        before = lax.ppermute(last, axis, up)
        after = lax.ppermute(first, axis, down)
        shard = jnp.concatenate([before, shard, after], axis=dim)
    return shard


def fourier_table():
    orders = jnp.arange(LMAX, dtype=jnp.int32)
    places = jnp.arange(NLON, dtype=jnp.int32)
    phases = orders[:, None] * places[None, :] % NLON
    angles = phases.astype(jnp.float32) * (2.0 * math.pi / NLON)
    weight = jnp.where(orders == 0, 1.0, 2.0).astype(jnp.float32)[:, None]
    return jnp.concatenate([weight * jnp.cos(angles), -weight * jnp.sin(angles)], axis=0)


def per_device(spectrum, legendre, block_slots, kernel_values, near_rows, mix_weights):
    lat_count = lax.axis_size("lat")
    lat_index = lax.axis_index("lat")
    ch_index = lax.axis_index("ch")
    row_count = legendre.shape[0]
    chan_dev = spectrum.shape[1]
    northern = lat_index < lat_count // 2
    parity = jnp.where(northern, 0, 1).astype(jnp.int32)
    zero_sum = jnp.zeros((row_count, chan_dev, 2, LMAX), jnp.float32)
    chosen = lax.dynamic_index_in_dim(
        lax.all_gather(spectrum, "lat", axis=0, tiled=True), parity, 2, keepdims=False
    )
    slot_rows = jnp.arange(chosen.shape[0], dtype=jnp.int32)
    order_ids = block_slots[slot_rows // ORDER_BLOCK] * ORDER_BLOCK + slot_rows % ORDER_BLOCK
    columns = jnp.take(legendre, order_ids, axis=2)
    contribution = jnp.einsum("rkn,ncxk->rcxn", columns, chosen, preferred_element_type=jnp.float32)
    partial_sum = zero_sum.at[:, :, :, order_ids].add(contribution)
    split_sums = partial_sum.reshape(row_count, chan_dev, 2, lat_count, LMAX // lat_count)
    by_source = lax.all_to_all(split_sums, "lat", split_axis=3, concat_axis=3, tiled=True)
    flipped = by_source[:, :, :, ::-1]
    returned = lax.all_to_all(flipped, "lat", split_axis=3, concat_axis=3, tiled=True)
    mirrored = returned.reshape(row_count, chan_dev, 2, LMAX)
    mirror_sign = jnp.where(northern, -1.0, 1.0).astype(jnp.float32)
    spectral = partial_sum + mirror_sign * mirrored[::-1]
    grid_field = jnp.dot(
        spectral.reshape(row_count * chan_dev, 2 * LMAX),
        fourier_table(),
        precision=lax.Precision.HIGHEST,
        preferred_element_type=jnp.float32,
    )
    grid_field = grid_field.reshape(row_count, chan_dev, NLON).astype(jnp.bfloat16)
    local_rows = near_rows - (lat_index * row_count - REACH)
    padded = padded_2(grid_field, (("lat", 0),), REACH)
    gathered = jnp.take(padded, local_rows, axis=0)
    spread = jnp.zeros((KER, row_count, chan_dev, NLON), jnp.float32)
    for offset in range(TAPS):
        rolled = jnp.roll(gathered, LON_REACH - offset, axis=3)
        spread = spread + jnp.einsum(
            "kiq,iqcx->kicx",
            kernel_values[:, :, :, offset],
            rolled,
            preferred_element_type=jnp.float32,
        )
    own_weights = lax.dynamic_slice_in_dim(mix_weights, ch_index * chan_dev, chan_dev, 1)
    weight_cols = own_weights.astype(jnp.float32)
    return lax.psum_scatter(
        jnp.einsum("kcd,kicx->dix", weight_cols, spread, precision=lax.Precision.HIGHEST),
        "ch",
        scatter_dimension=0,
        tiled=True,
    ).astype(jnp.bfloat16)


def solution(mesh):
    return jax.shard_map(
        per_device,
        mesh=mesh,
        in_specs=(
            P("lat", "ch", None, None, None),
            P("lat", None, None),
            P(),
            P(None, "lat", None, None),
            P("lat", None),
            P(),
        ),
        out_specs=P("ch", "lat", None),
        check_vma=False,
    )
```

profile of v0, /device:TPU:1, one launch (start us, length us, event | category | flops | bytes accessed | tf_op | source)
XLA Modules:
  0.0 490.7 jit_solution(12187650134679098284)
XLA Ops:
  8.3 8.9 %copy.18 = bf16[20,256,512]{1,0,2:T(8,128)(2,1)} copy(bf16[20,256,512]{2,1,0:T(8,128)(2,1)} %param.7) | data formatting | bytes 10485760 | tf_op args[1]
  18.8 4.5 compare_select_fusion.3
  24.0 16.1 %compare_and_fusion.1 = (pred[512]{0:T(512)(128)(4,1)S(1)}, s32[512]{0:T(512)S(1)}) fusion(pred[512]{0:T(512)(128)(4,1)S(1)} %compare_reduce_fusion, pred[512]{0:T(512)(128)(4,1)S(1)} %compare_reduce_fusion.1, pred[512]{0:T(512)(128)(4,1)S(1)} %compare_reduce_fusion.2, pred[512]{0:T(512)(128)(4,1)S(1)} %compare_reduce_fusion.3, ...), kind=kLoop, calls=%fused_computation.126 | loop fusion | flops 19968 | bytes 17508 | tf_op jit(solution)/shard_map/jit(_take)/and | solution.py:52
  40.2 6.4 %gather_fusion = bf16[512,20,256]{2,1,0:T(8,128)(2,1)} fusion(bf16[20,256,512]{1,0,2:T(8,128)(2,1)} %copy.18, s32[1024]{0:T(1024)S(1)} %pad_clamp_fusion.1), kind=kCustom, calls=%fused_computation | custom fusion | bytes 10487808 | tf_op jit(solution)/shard_map/jit(_take)/gather | solution.py:52
  46.6 39.5 %all-gather.2.cloned.1.call-done = bf16[512,8,2,2,256]{4,1,3,2,0:T(8,128)(2,1)} async-done(((bf16[16,8,2,2,256]{4,1,3,2,0:T(8,128)(2,1)}), bf16[512,8,2,2,256]{4,1,3,2,0:T(8,128)(2,1)}) %all-gather.2.cloned.1.call-update) | async-done | bytes 8388624 | tf_op jit(solution)/shard_map/all_gather | solution.py:48
  86.1 7.8 %fusion = f32[512,20,8,2]{1,2,3,0:T(8,128)} fusion(bf16[512,20,256]{2,1,0:T(8,128)(2,1)} %gather_fusion, pred[512]{0:T(512)(128)(4,1)S(1)} %get-tuple-element.7, bf16[512,8,2,2,256]{4,1,3,2,0:T(8,128)(2,1)} %all-gather.2.cloned.1.call-done, s32[]{:T(128)S(6)} %select_n.109), kind=kOutput, calls=%fused_computation.3 | convolution fusion | flops 86507520 | bytes 11141636 | tf_op jit(solution)/shard_map/rkn,ncxk->rcxn/dot_general | solution.py:53
  96.1 61.8 %scatter_fusion = f32[20,8,2,512]{0,1,3,2:T(8,128)} fusion(f32[20,8,2,512]{0,1,3,2:T(8,128)} %broadcast_in_dim.39, s32[512]{0:T(512)S(1)} %bitcast.115, f32[512,20,8,2]{1,2,3,0:T(8,128)} %fusion), kind=kCustom, calls=%fused_computation.2 | custom fusion | flops 163840 | bytes 1968128 | tf_op jit(solution)/shard_map/scatter-add | solution.py:54
  157.9 4.7 copy.60
  162.5 6.5 %reshape.292 = f32[32,1,5120]{2,1,0:T(1,128)} reshape(f32[32,2,16,8,20]{4,3,2,1,0:T(8,128)} %bitcast.113) | data formatting | bytes 1310720
  169.0 6.6 %all-to-all-start = ((f32[32,1,5120]{2,1,0:T(1,128)}), f32[32,1,5120]{2,1,0:T(1,128)S(1)}, u32[]{:S(2)}, u32[]{:S(2)}) async-start(f32[32,1,5120]{2,1,0:T(1,128)} %reshape.292), calls=%async_computation | async-start | bytes 1310720 | tf_op jit(solution)/shard_map/all_to_all | solution.py:56
  175.6 18.8 %all-to-all-done = f32[32,1,5120]{2,1,0:T(1,128)S(1)} async-done(((f32[32,1,5120]{2,1,0:T(1,128)}), f32[32,1,5120]{2,1,0:T(1,128)S(1)}, u32[]{:S(2)}, u32[]{:S(2)}) %all-to-all-start) | async-done | bytes 655392 | tf_op jit(solution)/shard_map/all_to_all | solution.py:56
  197.1 6.2 %reshape.293 = f32[32,2,16,8,20]{4,3,2,1,0:T(8,128)} reshape(f32[32,5120]{1,0:T(8,128)S(1)} %reduce.50) | data formatting | bytes 1310720
  203.3 4.7 reverse_bitcast_fusion
  208.0 6.5 %reshape.294 = f32[32,1,5120]{2,1,0:T(1,128)} reshape(f32[32,2,16,8,20]{4,3,2,1,0:T(8,128)} %reverse_bitcast_fusion) | data formatting | bytes 1310720
  214.5 6.4 %all-to-all-start.1 = ((f32[32,1,5120]{2,1,0:T(1,128)}), f32[32,1,5120]{2,1,0:T(1,128)}, u32[]{:S(2)}, u32[]{:S(2)}) async-start(f32[32,1,5120]{2,1,0:T(1,128)} %reshape.294), calls=%async_computation.1 | async-start | bytes 1310720 | tf_op jit(solution)/shard_map/all_to_all | solution.py:58
  222.4 13.3 %sine_multiply_fusion = (f32[512,1440]{0,1:T(8,128)S(1)}, f32[512,1440]{0,1:T(8,128)}) fusion(f32[512]{0:T(512)S(1)} %fusion.66, f32[512]{0:T(512)S(1)} %fusion.65), kind=kLoop, calls=%fused_computation.54 | loop fusion | flops 8110080 | bytes 5902336 | tf_op jit(solution)/shard_map/mul | solution.py:35
  235.7 4.3 all-to-all-done.1
  240.0 4.2 reduce.51
  244.2 7.2 %reshape.295 = f32[32,2,16,8,20]{4,3,2,1,0:T(8,128)} reshape(f32[32,5120]{1,0:T(8,128)} %reduce.51) | data formatting | bytes 1310720
  251.4 4.7 copy.21
  256.1 7.3 %rev.7 = f32[20,8,2,512]{0,1,3,2:T(8,128)} reverse(f32[20,8,2,512]{0,1,3,2:T(8,128)} %bitcast.112), dimensions={0} | reverse | bytes 1310720 | tf_op jit(solution)/shard_map/rev | solution.py:61
  263.3 5.8 %multiply_add_fusion = f32[20,8,2,512]{0,1,3,2:T(8,128)} fusion(f32[20,8,2,512]{0,1,3,2:T(8,128)} %scatter_fusion, f32[20,8,2,512]{0,1,3,2:T(8,128)} %rev.7, f32[]{:T(128)S(6)} %select_n.113), kind=kLoop, calls=%fused_computation.14 | loop fusion | flops 327680 | bytes 1966084 | tf_op jit(solution)/shard_map/add | solution.py:61
  273.0 7.5 %fusion.48 = bf16[20,8,1440]{2,1,0:T(8,128)(2,1)S(1)} fusion(f32[20,8,1024]{2,1,0:T(8,128)} %copy.22, f32[512,1440]{0,1:T(8,128)S(1)} %get-tuple-element.68, f32[512,1440]{0,1:T(8,128)} %get-tuple-element.69), kind=kOutput, calls=%fused_computation.60 | convolution fusion | flops 2832860160 | bytes 7014400 | tf_op jit(solution)/shard_map/dot_general | solution.py:62
  280.5 5.1 %collective-permute-start = (bf16[2,8,1440]{2,1,0:T(8,128)(2,1)S(1)}, bf16[2,8,1440]{2,1,0:T(8,128)(2,1)S(1)}, u32[]{:S(2)}, u32[]{:S(2)}) collective-permute-start(bf16[2,8,1440]{2,1,0:T(8,128)(2,1)S(1)} %get-tuple-element.25), channel_id=1, source_target_pairs={{0,8},{8,16},{16,24},{24,32},{32,40},{40,48},{48,56},{56,64},{64,7... | collective-permute-start | bytes 138248 | tf_op jit(solution)/shard_map/ppermute | solution.py:23
  300.0 4.2 fusion.86
  304.2 4.2 fusion.84
  316.9 5.2 %fusion.25 = f32[20,8,1440,3]{2,3,1,0:T(4,128)} fusion(bf16[20,6,8,1]{3,1,2,0:T(8,128)(2,1)S(1)} %get-tuple-element.22, bf16[20,6,8,1439]{3,1,2,0:T(8,128)(2,1)} %get-tuple-element.24, bf16[3,20,6,1]{2,0,1,3:T(4,128)(2,1)S(1)} %copy-done.4), kind=kOutput, calls=%fused_computation.32 | convolution fusion | flops 13824000 | bytes 5530320 | tf_op jit(solution)/shard_map/kiq,iqcx->kicx/dot_general | solution.py:75
  322.1 5.5 %fusion.17 = f32[20,8,1440,3]{2,3,1,0:T(4,128)} fusion(bf16[20,6,8,1438]{3,1,2,0:T(8,128)(2,1)} %get-tuple-element.19, bf16[20,6,8,2]{3,1,2,0:T(8,128)(2,1)S(1)} %get-tuple-element.17, bf16[3,20,6,1]{2,0,1,3:T(4,128)(2,1)S(1)} %copy-done.5), kind=kOutput, calls=%fused_computation.24 | convolution fusion | flops 13824000 | bytes 5530320 | tf_op jit(solution)/shard_map/kiq,iqcx->kicx/dot_general | solution.py:75
  327.6 5.3 %fusion.29 = f32[20,8,1440,3]{2,3,1,0:T(4,128)} fusion(bf16[20,6,8,2]{3,1,2,0:T(8,128)(2,1)S(1)} %get-tuple-element.18, bf16[20,6,8,1438]{3,1,2,0:T(8,128)(2,1)} %get-tuple-element.20, bf16[3,20,6,1]{2,0,1,3:T(4,128)(2,1)S(1)} %copy-done.2), kind=kOutput, calls=%fused_computation.36 | convolution fusion | flops 13824000 | bytes 5530320 | tf_op jit(solution)/shard_map/kiq,iqcx->kicx/dot_general | solution.py:75
  346.0 13.6 %add_bitcast_fusion = f32[3,20,8,1440]{3,0,2,1:T(4,128)} fusion(f32[20,8,1440,3]{2,3,1,0:T(4,128)} %fusion.37, f32[20,8,1440,3]{2,3,1,0:T(4,128)} %fusion.33, f32[20,8,1440,3]{2,3,1,0:T(4,128)} %fusion.29, f32[20,8,1440,3]{2,3,1,0:T(4,128)} %fusion.25, f32[20,8,1440,3]{2,3,1,0:T(4,128)S(1)} %fusion.21, f32[20,8,1440,3]{2,3,1,0:T(4,128)} %fusion.17, ...), kind=kOutput, calls=%fused_computation.49 | convolution fusion | flops 15206400 | bytes 27648840 | tf_op jit(solution)/shard_map/kiq,iqcx->kicx/dot_general | solution.py:75
  359.6 8.7 %convolution_bitcast_fusion = f32[64,20,1440]{2,0,1:T(8,128)} fusion(f32[3,20,8,1440]{3,0,2,1:T(4,128)} %add_bitcast_fusion, bf16[3,64,64]{2,1,0:T(8,128)(2,1)S(1)} %copy-done, s32[]{:T(128)S(6)} %select_n.103), kind=kOutput, calls=%fused_computation.11 | convolution fusion | flops 530841600 | bytes 10143748 | tf_op jit(solution)/shard_map/kcd,kicx->dix/dot_general | solution.py:84
  368.3 113.0 %reduce-scatter.2.cloned.1.call-done = f32[8,20,1440]{2,0,1:T(8,128)} async-done(((f32[64,20,1440]{2,0,1:T(8,128)}), f32[8,20,1440]{2,0,1:T(8,128)}) %reduce-scatter.2.cloned.1.call-update) | async-done | bytes 921616 | tf_op jit(solution)/shard_map/reduce_scatter | solution.py:83
  (98 shorter events, 52.0 us)
Async XLA Ops:
  6.5 353.1 %copy-start = (bf16[3,64,64]{2,1,0:T(8,128)(2,1)S(1)}, bf16[3,64,64]{2,1,0:T(8,128)(2,1)}, u32[]{:S(2)}) copy-start(bf16[3,64,64]{2,1,0:T(8,128)(2,1)} %param.11) | copy-start | bytes 73732
  6.5 79.5 %all-gather.2.cloned.1.call-start = ((), (), s32[]{:S(2)}) async-start(), calls=%async_computation.3 | async-start | bytes 8650752 | tf_op jit(solution)/shard_map/all_gather | solution.py:48
  8.3 9.8 %copy-start.1 = (s32[32]{0:T(128)S(1)}, s32[32]{0:T(128)}, u32[]{:S(2)}) copy-start(s32[32]{0:T(128)} %param.8) | copy-start | bytes 388
  169.0 25.4 %all-to-all-start = ((f32[32,1,5120]{2,1,0:T(1,128)}), f32[32,1,5120]{2,1,0:T(1,128)S(1)}, u32[]{:S(2)}, u32[]{:S(2)}) async-start(f32[32,1,5120]{2,1,0:T(1,128)} %reshape.292), calls=%async_computation | async-start | bytes 1310720 | tf_op jit(solution)/shard_map/all_to_all | solution.py:56
  208.0 13.1 %copy-start.10 = (s32[20,6]{0,1:T(8,128)S(1)}, s32[20,6]{0,1:T(8,128)}, u32[]{:S(2)}) copy-start(s32[20,6]{0,1:T(8,128)} %param.10) | copy-start | bytes 1444
  208.0 13.8 %copy-start.8 = (bf16[3,20,6,9]{1,2,3,0:T(8,128)(2,1)S(1)}, bf16[3,20,6,9]{1,2,3,0:T(8,128)(2,1)}, u32[]{:S(2)}) copy-start(bf16[3,20,6,9]{1,2,3,0:T(8,128)(2,1)} %param.9) | copy-start | bytes 19444
  214.5 25.6 %all-to-all-start.1 = ((f32[32,1,5120]{2,1,0:T(1,128)}), f32[32,1,5120]{2,1,0:T(1,128)}, u32[]{:S(2)}, u32[]{:S(2)}) async-start(f32[32,1,5120]{2,1,0:T(1,128)} %reshape.294), calls=%async_computation.1 | async-start | bytes 1310720 | tf_op jit(solution)/shard_map/all_to_all | solution.py:58
  220.9 260.5 %reduce-scatter.2.cloned.1.call-start = ((), (), s32[]{:S(2)}) async-start(), calls=%async_computation.4 | async-start | bytes 8847360 | tf_op jit(solution)/shard_map/reduce_scatter | solution.py:83
  273.0 14.8 %copy-start.11 = (s32[120]{0:T(128)S(1)}, s32[120]{0:T(128)}, u32[]{:S(2)}) copy-start(s32[120]{0:T(128)} %reshape.161) | copy-start | bytes 1444
  280.5 14.8 %collective-permute-start = (bf16[2,8,1440]{2,1,0:T(8,128)(2,1)S(1)}, bf16[2,8,1440]{2,1,0:T(8,128)(2,1)S(1)}, u32[]{:S(2)}, u32[]{:S(2)}) collective-permute-start(bf16[2,8,1440]{2,1,0:T(8,128)(2,1)S(1)} %get-tuple-element.25), channel_id=1, source_target_pairs={{0,8},{8,16},{16,24},{24,32},{32,40},{40,48},{48,56},{56,64},{64,7... | collective-permute-start | bytes 138248 | tf_op jit(solution)/shard_map/ppermute | solution.py:23
  285.6 9.7 %collective-permute-start.1 = (bf16[2,8,1440]{2,1,0:T(8,128)(2,1)S(1)}, bf16[2,8,1440]{2,1,0:T(8,128)(2,1)S(1)}, u32[]{:S(2)}, u32[]{:S(2)}) collective-permute-start(bf16[2,8,1440]{2,1,0:T(8,128)(2,1)S(1)} %get-tuple-element.26), channel_id=1, source_target_pairs={{8,0},{16,8},{24,16},{32,24},{40,32},{48,40},{56,48},{64,56},{72,6... | collective-permute-start | bytes 138248 | tf_op jit(solution)/shard_map/ppermute | solution.py:24
  296.2 1.9 copy-start.9
  310.7 2.6 copy-start.6
  313.3 3.6 copy-start.4
  316.9 5.2 %copy-start.5 = (bf16[3,20,6,1]{2,0,1,3:T(4,128)(2,1)S(1)}, bf16[3,20,6,1]{2,0,1,3:T(4,128)(2,1)}, u32[]{:S(2)}) copy-start(bf16[3,20,6,1]{2,0,1,3:T(4,128)(2,1)} %copy.48) | copy-start | bytes 2164
  322.1 5.5 %copy-start.2 = (bf16[3,20,6,1]{2,0,1,3:T(4,128)(2,1)S(1)}, bf16[3,20,6,1]{2,0,1,3:T(4,128)(2,1)}, u32[]{:S(2)}) copy-start(bf16[3,20,6,1]{2,0,1,3:T(4,128)(2,1)} %copy.52) | copy-start | bytes 2164
  327.6 5.3 %copy-start.3 = (bf16[3,20,6,1]{2,0,1,3:T(4,128)(2,1)S(1)}, bf16[3,20,6,1]{2,0,1,3:T(4,128)(2,1)}, u32[]{:S(2)}) copy-start(bf16[3,20,6,1]{2,0,1,3:T(4,128)(2,1)} %copy.47) | copy-start | bytes 2164
  342.8 3.2 copy-start.7
Sparse Core Ops, SparseCore 0:
  9.2 76.7 all-gather.1
  368.5 112.8 reduce-scatter.1
where the time goes:
time: 499 us; the launch traced here: 491 us
  waiting for transfers between devices  176 us (35%)
  other arithmetic  113 us (23%)
  local copies, waits for them, and re-layouts  97.3 us (19%)
  matrix products  70.3 us (14%)
  starting transfers between devices  20.4 us (4%)
  between operations  14.2 us (3%)
    reduce_scatter x1, waiting for transfers between devices, per_device(): lax.psum_scatter(jnp.einsum('kcd,kicx->dix', weight_cols, spread, precisi...  113 us
    scatter-add x1, other arithmetic, per_device(): partial_sum = zero_sum.at[:, :, :, order_ids].add(contribution)  61.8 us
    unnamed x40, local copies, waits for them, and re-layouts  48.5 us
    dot_general x9, matrix products, per_device(): jnp.einsum('kiq,iqcx->kicx', kernel_values[:, :, :, offset], rolled, pref...  46.3 us
    all_gather x1, waiting for transfers between devices, per_device(): lax.all_gather(spectrum, 'lat', axis=0, tiled=True)  39.5 us
    all_to_all x1, waiting for transfers between devices, per_device(): lax.all_to_all(split_sums, 'lat', split_axis=3, concat_axis=3, tiled=True)  18.8 us
    and x1, other arithmetic, per_device(): columns = jnp.take(legendre, order_ids, axis=2)  16.1 us
    slice x8, local copies, waits for them, and re-layouts, per_device(): rolled = jnp.roll(gathered, LON_REACH - offset, axis=3)  14 us
  transfers between devices with their start and end apart: 6, of which 4 were waited for; matrix products, arithmetic and copies ran while one was open for 12% of the time, Pallas kernels for 0%

commit v1 on v0

--- a/solution.py
+++ b/solution.py
@@ -11,6 +11,13 @@
 REACH = 2
 LON_REACH = 4
 TAPS = 9
+
+
+def exchange_gather(shard, axis, along):
+    size = lax.axis_size(axis)
+    parts = jnp.stack([shard for _ in range(size)])
+    parts = lax.all_to_all(parts, axis, split_axis=0, concat_axis=0)
+    return jnp.concatenate(parts, axis=along)
 
 
 def padded_2(shard, sides, width):
@@ -45,7 +52,7 @@
     parity = jnp.where(northern, 0, 1).astype(jnp.int32)
     zero_sum = jnp.zeros((row_count, chan_dev, 2, LMAX), jnp.float32)
     chosen = lax.dynamic_index_in_dim(
-        lax.all_gather(spectrum, "lat", axis=0, tiled=True), parity, 2, keepdims=False
+        exchange_gather(spectrum, "lat", 0), parity, 2, keepdims=False
     )
     slot_rows = jnp.arange(chosen.shape[0], dtype=jnp.int32)
     order_ids = block_slots[slot_rows // ORDER_BLOCK] * ORDER_BLOCK + slot_rows % ORDER_BLOCK

time: 499 us -> 630 us (1.26)
  waiting for transfers between devices: 176 us -> 283 us
  starting transfers between devices: 20.4 us -> 35.8 us
  local copies, waits for them, and re-layouts: 97.3 us -> 108 us
    all_to_all x0 -> x1, waiting for transfers between devices: none -> 147 us  [exchange_gather(): parts = lax.all_to_all(parts, axis, split_axis=0, concat_axis=0)]
    all_gather x1 -> x0, waiting for transfers between devices: 39.5 us -> none  [per_device(): lax.all_gather(spectrum, 'lat', axis=0, tiled=True)]
    all_to_all x0 -> x1, starting transfers between devices: none -> 11.1 us  [exchange_gather(): parts = lax.all_to_all(parts, axis, split_axis=0, concat_axis=0)]
    all_to_all x0 -> x1, local copies, waits for them, and re-layouts: none -> 7.83 us  [exchange_gather(): parts = lax.all_to_all(parts, axis, split_axis=0, concat_axis=0)]
    unnamed x40 -> x42, local copies, waits for them, and re-layouts: 48.5 us -> 47.6 us
  transfers between devices with their start and end apart: 6 -> 6, of which waited for: 4 -> 4; matrix products, arithmetic and copies ran while one was open for 12% -> 10% of each run, Pallas kernels for 0% -> 0%
where the time goes in v1:
time: 630 us; the launch traced here: 622 us
  waiting for transfers between devices  283 us (45%)
  other arithmetic  112 us (18%)
  local copies, waits for them, and re-layouts  108 us (17%)
  matrix products  67.6 us (11%)
  starting transfers between devices  35.8 us (6%)
  between operations  14.2 us (2%)
    all_to_all x1, waiting for transfers between devices, exchange_gather(): parts = lax.all_to_all(parts, axis, split_axis=0, concat_axis=0)  147 us
    reduce_scatter x1, waiting for transfers between devices, per_device(): lax.psum_scatter(jnp.einsum('kcd,kicx->dix', weight_cols, spread, precisi...  114 us
    scatter-add x1, other arithmetic, per_device(): partial_sum = zero_sum.at[:, :, :, order_ids].add(contribution)  61.8 us
    unnamed x42, local copies, waits for them, and re-layouts  47.6 us
    dot_general x9, matrix products, per_device(): jnp.einsum('kiq,iqcx->kicx', kernel_values[:, :, :, offset], rolled, pref...  46.3 us
    all_to_all x1, waiting for transfers between devices, per_device(): lax.all_to_all(split_sums, 'lat', split_axis=3, concat_axis=3, tiled=True)  18.8 us
    and x1, other arithmetic, per_device(): columns = jnp.take(legendre, order_ids, axis=2)  15.6 us
    slice x8, local copies, waits for them, and re-layouts, per_device(): rolled = jnp.roll(gathered, LON_REACH - offset, axis=3)  14 us
  transfers between devices with their start and end apart: 6, of which 4 were waited for; matrix products, arithmetic and copies ran while one was open for 10% of the time, Pallas kernels for 0%

profile of v1, /device:TPU:1, one launch (start us, length us, event | category | flops | bytes accessed | tf_op | source)
XLA Modules:
  0.0 621.5 jit_solution(7775017970923469442)
XLA Ops:
  7.5 4.2 stack.2
  11.8 11.1 %all-to-all-start = ((bf16[32,16,8,2,2,256]{5,2,4,1,3,0:T(8,128)(2,1)}), bf16[32,16,8,2,2,256]{5,2,4,1,3,0:T(8,128)(2,1)}, u32[]{:S(2)}, u32[]{:S(2)}) async-start(bf16[32,16,8,2,2,256]{5,2,4,1,3,0:T(8,128)(2,1)} %stack.2), calls=%async_computation | async-start | bytes 16777216 | tf_op jit(solution)/shard_map/all_to_all | solution.py:19
  22.9 8.9 %copy.36 = bf16[20,256,512]{1,0,2:T(8,128)(2,1)} copy(bf16[20,256,512]{2,1,0:T(8,128)(2,1)} %param.7) | data formatting | bytes 10485760 | tf_op args[1]
  33.3 4.3 compare_select_fusion.3
  38.3 15.6 %compare_and_fusion.1 = (pred[512]{0:T(512)(128)(4,1)S(1)}, s32[512]{0:T(512)S(1)}) fusion(pred[512]{0:T(512)(128)(4,1)S(1)} %compare_reduce_fusion, pred[512]{0:T(512)(128)(4,1)S(1)} %compare_reduce_fusion.1, pred[512]{0:T(512)(128)(4,1)S(1)} %compare_reduce_fusion.2, pred[512]{0:T(512)(128)(4,1)S(1)} %compare_reduce_fusion.3, ...), kind=kLoop, calls=%fused_computation.126 | loop fusion | flops 19968 | bytes 17508 | tf_op jit(solution)/shard_map/jit(_take)/and | solution.py:59
  53.9 6.4 %gather_fusion = bf16[512,20,256]{2,1,0:T(8,128)(2,1)} fusion(bf16[20,256,512]{1,0,2:T(8,128)(2,1)} %copy.36, s32[1024]{0:T(1024)S(1)} %pad_clamp_fusion.1), kind=kCustom, calls=%fused_computation | custom fusion | bytes 10487808 | tf_op jit(solution)/shard_map/jit(_take)/gather | solution.py:59
  60.4 146.6 %all-to-all-done = bf16[32,16,8,2,2,256]{5,2,4,1,3,0:T(8,128)(2,1)} async-done(((bf16[32,16,8,2,2,256]{5,2,4,1,3,0:T(8,128)(2,1)}), bf16[32,16,8,2,2,256]{5,2,4,1,3,0:T(8,128)(2,1)}, u32[]{:S(2)}, u32[]{:S(2)}) %all-to-all-start) | async-done | bytes 8388640 | tf_op jit(solution)/shard_map/all_to_all | solution.py:19
  206.9 7.8 %copy.38 = bf16[32,16,8,2,2,256]{5,2,4,3,1,0:T(8,128)(2,1)} copy(bf16[32,16,8,2,2,256]{5,2,4,1,3,0:T(8,128)(2,1)} %all-to-all-done) | data formatting | bytes 16777216 | tf_op jit(solution)/shard_map/all_to_all | solution.py:19
  214.8 5.1 fusion
  222.1 61.8 %scatter_fusion = f32[20,8,2,512]{0,1,3,2:T(8,128)} fusion(f32[20,8,2,512]{0,1,3,2:T(8,128)} %broadcast_in_dim.39, s32[512]{0:T(512)S(1)} %bitcast.117, f32[512,20,8,2]{1,2,3,0:T(8,128)} %fusion), kind=kCustom, calls=%fused_computation.2 | custom fusion | flops 163840 | bytes 1968128 | tf_op jit(solution)/shard_map/scatter-add | solution.py:61
  283.9 4.6 copy.79
  288.5 6.5 %reshape.298 = f32[32,1,5120]{2,1,0:T(1,128)} reshape(f32[32,2,16,8,20]{4,3,2,1,0:T(8,128)} %bitcast.114) | data formatting | bytes 1310720
  294.9 10.9 %all-to-all-start.1 = ((f32[32,1,5120]{2,1,0:T(1,128)}), f32[32,1,5120]{2,1,0:T(1,128)S(1)}, u32[]{:S(2)}, u32[]{:S(2)}) async-start(f32[32,1,5120]{2,1,0:T(1,128)} %reshape.298), calls=%async_computation.1 | async-start | bytes 1310720 | tf_op jit(solution)/shard_map/all_to_all | solution.py:63
  305.9 18.8 %all-to-all-done.1 = f32[32,1,5120]{2,1,0:T(1,128)S(1)} async-done(((f32[32,1,5120]{2,1,0:T(1,128)}), f32[32,1,5120]{2,1,0:T(1,128)S(1)}, u32[]{:S(2)}, u32[]{:S(2)}) %all-to-all-start.1) | async-done | bytes 655392 | tf_op jit(solution)/shard_map/all_to_all | solution.py:63
  327.4 6.2 reshape.299
  333.6 4.6 reverse_bitcast_fusion
  338.2 6.5 %reshape.300 = f32[32,1,5120]{2,1,0:T(1,128)} reshape(f32[32,2,16,8,20]{4,3,2,1,0:T(8,128)} %reverse_bitcast_fusion) | data formatting | bytes 1310720
  344.7 6.4 %all-to-all-start.2 = ((f32[32,1,5120]{2,1,0:T(1,128)}), f32[32,1,5120]{2,1,0:T(1,128)}, u32[]{:S(2)}, u32[]{:S(2)}) async-start(f32[32,1,5120]{2,1,0:T(1,128)} %reshape.300), calls=%async_computation.2 | async-start | bytes 1310720 | tf_op jit(solution)/shard_map/all_to_all | solution.py:65
  352.6 13.3 %sine_multiply_fusion = (f32[512,1440]{0,1:T(8,128)S(1)}, f32[512,1440]{0,1:T(8,128)}) fusion(f32[512]{0:T(512)S(1)} %fusion.66, f32[512]{0:T(512)S(1)} %fusion.65), kind=kLoop, calls=%fused_computation.54 | loop fusion | flops 8110080 | bytes 5902336 | tf_op jit(solution)/shard_map/mul | solution.py:42
  365.9 4.3 all-to-all-done.2
  374.4 7.1 %reshape.301 = f32[32,2,16,8,20]{4,3,2,1,0:T(8,128)} reshape(f32[32,5120]{1,0:T(8,128)} %reduce.51) | data formatting | bytes 1310720
  381.6 4.7 copy.40
  386.2 7.2 %rev.7 = f32[20,8,2,512]{0,1,3,2:T(8,128)} reverse(f32[20,8,2,512]{0,1,3,2:T(8,128)} %bitcast.113), dimensions={0} | reverse | bytes 1310720 | tf_op jit(solution)/shard_map/rev | solution.py:68
  393.5 5.8 multiply_add_fusion
  403.1 7.5 %fusion.48 = bf16[20,8,1440]{2,1,0:T(8,128)(2,1)S(1)} fusion(f32[20,8,1024]{2,1,0:T(8,128)} %copy.41, f32[512,1440]{0,1:T(8,128)S(1)} %get-tuple-element.68, f32[512,1440]{0,1:T(8,128)} %get-tuple-element.69), kind=kOutput, calls=%fused_computation.60 | convolution fusion | flops 2832860160 | bytes 7014400 | tf_op jit(solution)/shard_map/dot_general | solution.py:69
  410.6 5.1 collective-permute-start
  447.0 5.2 fusion.25
  452.2 5.5 fusion.17
  457.7 5.3 fusion.29
  476.0 13.6 %add_bitcast_fusion = f32[3,20,8,1440]{3,0,2,1:T(4,128)} fusion(f32[20,8,1440,3]{2,3,1,0:T(4,128)} %fusion.37, f32[20,8,1440,3]{2,3,1,0:T(4,128)} %fusion.33, f32[20,8,1440,3]{2,3,1,0:T(4,128)} %fusion.29, f32[20,8,1440,3]{2,3,1,0:T(4,128)} %fusion.25, f32[20,8,1440,3]{2,3,1,0:T(4,128)S(1)} %fusion.21, f32[20,8,1440,3]{2,3,1,0:T(4,128)} %fusion.17, ...), kind=kOutput, calls=%fused_computation.49 | convolution fusion | flops 15206400 | bytes 27648840 | tf_op jit(solution)/shard_map/kiq,iqcx->kicx/dot_general | solution.py:82
  489.7 8.7 %convolution_bitcast_fusion = f32[64,20,1440]{2,0,1:T(8,128)} fusion(f32[3,20,8,1440]{3,0,2,1:T(4,128)} %add_bitcast_fusion, bf16[3,64,64]{2,1,0:T(8,128)(2,1)S(1)} %copy-done, s32[]{:T(128)S(6)} %select_n.103), kind=kOutput, calls=%fused_computation.11 | convolution fusion | flops 530841600 | bytes 10143748 | tf_op jit(solution)/shard_map/kcd,kicx->dix/dot_general | solution.py:91
  498.4 113.7 %reduce-scatter.2.cloned.1.call-done = f32[8,20,1440]{2,0,1:T(8,128)} async-done(((f32[64,20,1440]{2,0,1:T(8,128)}), f32[8,20,1440]{2,0,1:T(8,128)}) %reduce-scatter.2.cloned.1.call-update) | async-done | bytes 921616 | tf_op jit(solution)/shard_map/reduce_scatter | solution.py:90
  (101 shorter events, 63.9 us)
Async XLA Ops:
  6.5 483.1 %copy-start = (bf16[3,64,64]{2,1,0:T(8,128)(2,1)S(1)}, bf16[3,64,64]{2,1,0:T(8,128)(2,1)}, u32[]{:S(2)}) copy-start(bf16[3,64,64]{2,1,0:T(8,128)(2,1)} %param.11) | copy-start | bytes 73732
  11.8 195.2 %all-to-all-start = ((bf16[32,16,8,2,2,256]{5,2,4,1,3,0:T(8,128)(2,1)}), bf16[32,16,8,2,2,256]{5,2,4,1,3,0:T(8,128)(2,1)}, u32[]{:S(2)}, u32[]{:S(2)}) async-start(bf16[32,16,8,2,2,256]{5,2,4,1,3,0:T(8,128)(2,1)} %stack.2), calls=%async_computation | async-start | bytes 16777216 | tf_op jit(solution)/shard_map/all_to_all | solution.py:19
  22.9 9.8 %copy-start.2 = (s32[32]{0:T(128)S(1)}, s32[32]{0:T(128)}, u32[]{:S(2)}) copy-start(s32[32]{0:T(128)} %param.8) | copy-start | bytes 388
  206.9 7.8 %copy-start.1 = (bf16[512,20,256]{2,1,0:T(8,128)(2,1)S(1)}, bf16[512,20,256]{2,1,0:T(8,128)(2,1)}, u32[]{:S(2)}) copy-start(bf16[512,20,256]{2,1,0:T(8,128)(2,1)} %gather_fusion) | copy-start | bytes 15728644
  294.9 29.7 %all-to-all-start.1 = ((f32[32,1,5120]{2,1,0:T(1,128)}), f32[32,1,5120]{2,1,0:T(1,128)S(1)}, u32[]{:S(2)}, u32[]{:S(2)}) async-start(f32[32,1,5120]{2,1,0:T(1,128)} %reshape.298), calls=%async_computation.1 | async-start | bytes 1310720 | tf_op jit(solution)/shard_map/all_to_all | solution.py:63
  338.2 13.1 %copy-start.11 = (s32[20,6]{0,1:T(8,128)S(1)}, s32[20,6]{0,1:T(8,128)}, u32[]{:S(2)}) copy-start(s32[20,6]{0,1:T(8,128)} %param.10) | copy-start | bytes 1444
  338.2 13.8 %copy-start.9 = (bf16[3,20,6,9]{1,2,3,0:T(8,128)(2,1)S(1)}, bf16[3,20,6,9]{1,2,3,0:T(8,128)(2,1)}, u32[]{:S(2)}) copy-start(bf16[3,20,6,9]{1,2,3,0:T(8,128)(2,1)} %param.9) | copy-start | bytes 19444
  344.7 25.6 %all-to-all-start.2 = ((f32[32,1,5120]{2,1,0:T(1,128)}), f32[32,1,5120]{2,1,0:T(1,128)}, u32[]{:S(2)}, u32[]{:S(2)}) async-start(f32[32,1,5120]{2,1,0:T(1,128)} %reshape.300), calls=%async_computation.2 | async-start | bytes 1310720 | tf_op jit(solution)/shard_map/all_to_all | solution.py:65
  351.0 261.1 %reduce-scatter.2.cloned.1.call-start = ((), (), s32[]{:S(2)}) async-start(), calls=%async_computation.4 | async-start | bytes 8847360 | tf_op jit(solution)/shard_map/reduce_scatter | solution.py:90
  403.1 14.8 %copy-start.12 = (s32[120]{0:T(128)S(1)}, s32[120]{0:T(128)}, u32[]{:S(2)}) copy-start(s32[120]{0:T(128)} %reshape.167) | copy-start | bytes 1444
  410.6 14.8 %collective-permute-start = (bf16[2,8,1440]{2,1,0:T(8,128)(2,1)S(1)}, bf16[2,8,1440]{2,1,0:T(8,128)(2,1)S(1)}, u32[]{:S(2)}, u32[]{:S(2)}) collective-permute-start(bf16[2,8,1440]{2,1,0:T(8,128)(2,1)S(1)} %get-tuple-element.25), channel_id=1, source_target_pairs={{0,8},{8,16},{16,24},{24,32},{32,40},{40,48},{48,56},{56,64},{64,7... | collective-permute-start | bytes 138248 | tf_op jit(solution)/shard_map/ppermute | solution.py:30
  415.7 9.7 %collective-permute-start.1 = (bf16[2,8,1440]{2,1,0:T(8,128)(2,1)S(1)}, bf16[2,8,1440]{2,1,0:T(8,128)(2,1)S(1)}, u32[]{:S(2)}, u32[]{:S(2)}) collective-permute-start(bf16[2,8,1440]{2,1,0:T(8,128)(2,1)S(1)} %get-tuple-element.26), channel_id=1, source_target_pairs={{8,0},{16,8},{24,16},{32,24},{40,32},{48,40},{56,48},{64,56},{72,6... | collective-permute-start | bytes 138248 | tf_op jit(solution)/shard_map/ppermute | solution.py:31
  426.2 1.9 copy-start.10
  440.8 2.6 copy-start.7
  443.3 3.6 copy-start.5
  446.9 5.2 copy-start.6
  452.2 5.5 copy-start.3
  457.7 5.3 copy-start.4
  472.9 3.2 copy-start.8
Sparse Core Ops, SparseCore 0:
  498.5 113.5 reduce-scatter.1
